TPU v7x, 32 devices: a whole 2x2x4 slice. The times are simulated.
32 devices in a mesh: rep: 2 (over y), shard: 16 (over z, x, core).
Axes of the slice: x: 2, y: 2, z: 4, core: 2. Of those that a mesh axis runs over, the one named last changes fastest.
Arguments:
- latents: bfloat16 [32, 128, 1152], P(('rep', 'shard')), may hold values from -5 to 5
- cond: float32 [32, 1152], P(('rep', 'shard')), may hold values from -6 to 6
- timesteps: int32 [32], P(('rep', 'shard')), may hold values from 0 to 999
- cotangent: bfloat16 [32, 128, 1152], P(('rep', 'shard')), may hold values from -6 to 6
- w_qkv: float32 [1152, 3456], P('shard'), may hold values from -0.11785113 to 0.11785113
- w_proj: float32 [1152, 1152], P('shard'), may hold values from -0.75 to 0.75
- w_fc1: float32 [1152, 4608], P('shard'), may hold values from -0.1875 to 0.1875
- w_fc2: float32 [4608, 1152], P('shard'), may hold values from -0.1875 to 0.1875
- w_ada: float32 [1152, 6912], P(None, 'shard'), may hold values from -0.015625 to 0.015625
- biases: float32 [16128], replicated, may hold values from -3 to 3
- m_qkv: float32 [1152, 3456], P('shard', 'rep'), may hold values from -0.00012272017 to 0.00012272017
- m_proj: float32 [1152, 1152], P('shard', 'rep'), may hold values from -0.00012272017 to 0.00012272017
- m_fc1: float32 [1152, 4608], P('shard', 'rep'), may hold values from -0.00012272017 to 0.00012272017
- m_fc2: float32 [4608, 1152], P('shard', 'rep'), may hold values from -0.00012272017 to 0.00012272017
- m_ada: float32 [1152, 6912], P('rep', 'shard'), may hold values from -0.00012272017 to 0.00012272017
- m_bias: float32 [16128], replicated, may hold values from -0.00012272017 to 0.00012272017
- v_qkv: float32 [1152, 3456], P('shard', 'rep'), may hold values from 4.1834e-11 to 1.67336e-10
- v_proj: float32 [1152, 1152], P('shard', 'rep'), may hold values from 4.1834e-11 to 1.67336e-10
- v_fc1: float32 [1152, 4608], P('shard', 'rep'), may hold values from 4.1834e-11 to 1.67336e-10
- v_fc2: float32 [4608, 1152], P('shard', 'rep'), may hold values from 4.1834e-11 to 1.67336e-10
- v_ada: float32 [1152, 6912], P('rep', 'shard'), may hold values from 4.1834e-11 to 1.67336e-10
- v_bias: float32 [16128], replicated, may hold values from 4.1834e-11 to 1.67336e-10
Outputs:
- block_out: float32 [32, 128, 1152], P(('rep', 'shard'))
- latents_grad: float32 [32, 128, 1152], P(('rep', 'shard'))
- cond_grad: float32 [32, 1152], P(('rep', 'shard'))
- new_qkv: float32 [1152, 3456], P('shard')
- new_proj: float32 [1152, 1152], P('shard')
- new_fc1: float32 [1152, 4608], P('shard')
- new_fc2: float32 [4608, 1152], P('shard')
- new_ada: float32 [1152, 6912], P(None, 'shard')
- bias_update: float32 [16128], replicated
- new_m_qkv: float32 [1152, 3456], P('shard', 'rep')
- new_m_proj: float32 [1152, 1152], P('shard', 'rep')
- new_m_fc1: float32 [1152, 4608], P('shard', 'rep')
- new_m_fc2: float32 [4608, 1152], P('shard', 'rep')
- new_m_ada: float32 [1152, 6912], P('rep', 'shard')
- new_m_bias: float32 [16128], replicated
- new_v_qkv: float32 [1152, 3456], P('shard', 'rep')
- new_v_proj: float32 [1152, 1152], P('shard', 'rep')
- new_v_fc1: float32 [1152, 4608], P('shard', 'rep')
- new_v_fc2: float32 [4608, 1152], P('shard', 'rep')
- new_v_ada: float32 [1152, 6912], P('rep', 'shard')
- new_v_bias: float32 [16128], replicated
All inputs are finite; a program needn't handle non-finite values.
Results may differ from a plain program's by a relative error of at most 0.014.
Values may be sent and summed in bfloat16 or wider, within the bound.
No kernel may reach another device: no remote copies, remote signals or barrier semaphores. Data moves between devices by JAX's collectives and lax.ppermute only.
A program may use at most 256 MiB of HBM per device.

v0:
```python
import math
import jax
import jax.numpy as jnp
from jax import lax
from jax.sharding import PartitionSpec as P

HD = 72
H = 16
FF = 4608
ln_eps = 1e-06
beta_one = 0.9
beta_two = 0.999
adam_eps = 1e-08
learn_rate = 0.03
decay_rate = 0.01
step_count = 2
gelu_coef = 0.044715


def product(form, left, right):
    return jnp.einsum(form, left, right, preferred_element_type=jnp.float32)


def normalize(rows):
    center = rows - jnp.mean(rows, axis=-1, keepdims=True)
    rstd = lax.rsqrt(jnp.mean(center * center, axis=-1, keepdims=True) + ln_eps)
    return (center * rstd, rstd)


def norm_back(grad, normed, rstd):
    return rstd * (
        grad
        - jnp.mean(grad, axis=-1, keepdims=True)
        - normed * jnp.mean(grad * normed, axis=-1, keepdims=True)
    )


def gelu_parts(pre):
    root = math.sqrt(2.0 / math.pi)
    inner = root * (pre + gelu_coef * pre * pre * pre)
    tangent = jnp.tanh(inner)
    value = 0.5 * pre * (1.0 + tangent)
    slope = 0.5 * (1.0 + tangent) + 0.5 * pre * (1.0 - tangent * tangent) * root * (
        1.0 + 3.0 * gelu_coef * pre * pre
    )
    return (value, slope)


def time_embed(steps, width):
    half = width // 2
    freqs = jnp.exp(-math.log(10000.0) * jnp.arange(half, dtype=jnp.float32) / half)
    angles = steps.astype(jnp.float32)[:, None] * freqs[None, :]
    return jnp.concatenate([jnp.cos(angles), jnp.sin(angles)], axis=1)


def adam_change(weight, grad, first, second, clip):
    scaled = grad * clip
    first_new = beta_one * first + (1.0 - beta_one) * scaled
    second_new = beta_two * second + (1.0 - beta_two) * scaled * scaled
    first_hat = first_new / (1.0 - beta_one**step_count)
    second_hat = second_new / (1.0 - beta_two**step_count)
    change = -learn_rate * (first_hat / (jnp.sqrt(second_hat) + adam_eps) + decay_rate * weight)
    return (change, first_new, second_new)


def shards(
    latents,
    cond,
    timesteps,
    cotangent,
    w_qkv,
    w_proj,
    w_fc1,
    w_fc2,
    w_ada,
    biases,
    m_qkv,
    m_proj,
    m_fc1,
    m_fc2,
    m_ada,
    m_bias,
    v_qkv,
    v_proj,
    v_fc1,
    v_fc2,
    v_ada,
    v_bias,
):
    axes = ("rep", "shard")
    replicas = lax.axis_size("rep")
    parts = lax.axis_size("shard")
    devices = replicas * parts
    rank = lax.axis_index("rep")
    turn = rank % 2
    couples = [(i, i ^ 1) for i in range(replicas)]
    length, width = latents.shape[1:]
    inner = H * HD
    half = inner // 2
    heads = H // 2
    rows = w_qkv.shape[0]
    folds = FF // (2 * width)
    unit = FF // (2 * parts * folds)

    def swap(value):
        return lax.ppermute(value, "rep", couples)

    def ordered(own, other, axis):
        first = jnp.concatenate([own, other], axis=axis)
        second = jnp.concatenate([other, own], axis=axis)
        return jnp.where(turn == 0, first, second)

    def own_half(value, axis):
        count = value.shape[axis] // 2
        return lax.dynamic_slice_in_dim(value, turn * count, count, axis)

    def spread(value):
        copies = jnp.broadcast_to(value, (devices,) + value.shape[1:])
        return lax.all_to_all(copies, axes, split_axis=0, concat_axis=0, tiled=True)

    b_q = own_half(biases[0:inner], 0)
    b_v = own_half(biases[inner : 2 * inner], 0)
    b_proj = biases[2 * inner : 2 * inner + width]
    b_fc1 = biases[2 * inner + width : 2 * inner + width + FF]
    b_fc2 = biases[2 * inner + width + FF : 2 * inner + 2 * width + FF]
    b_ada = biases[biases.shape[0] - 6 * width :]
    units = lax.dynamic_index_in_dim(b_fc1.reshape(parts, 2, folds, unit), turn, 1, keepdims=False)
    b_one = jnp.transpose(units, (1, 0, 2)).reshape(folds, width)
    wq_half = own_half(w_qkv.astype(jnp.bfloat16).reshape(rows, 3, inner), 2)
    pack_attn = jnp.concatenate(
        [w_proj.astype(jnp.bfloat16), wq_half.reshape(rows, 3 * half)], axis=1
    )
    full_attn = lax.all_gather(pack_attn, "shard", axis=0, tiled=True)
    wp_b = full_attn[:, :width]
    wq_b = full_attn[:, width:]
    w1_half = lax.dynamic_index_in_dim(
        w_fc1.astype(jnp.bfloat16).reshape(rows, parts, 2, folds, unit), turn, 2, keepdims=False
    )
    w1_half = jnp.transpose(w1_half, (0, 2, 1, 3)).reshape(rows, folds * width)
    w2_half = own_half(w_fc2.astype(jnp.bfloat16), 0).reshape(folds, rows, width)
    pack_mlp = jnp.concatenate([w1_half] + [w2_half[f] for f in range(folds)], axis=1)
    full_mlp = lax.all_gather(pack_mlp, "shard", axis=0, tiled=True)
    w1_b = [full_mlp[:, f * width : (f + 1) * width] for f in range(folds)]
    w2_b = [full_mlp[:, (folds + f) * width : (folds + f + 1) * width] for f in range(folds)]
    cvec = cond + time_embed(timesteps, width)
    silu_c = jax.nn.silu(cvec).astype(jnp.bfloat16)
    ada_local = w_ada.astype(jnp.bfloat16)
    silu_all = spread(silu_c)
    silu_group = lax.dynamic_slice_in_dim(silu_all, rank * parts, parts, 0)
    mod_cols = jnp.dot(silu_group, ada_local, preferred_element_type=jnp.float32)
    mod = lax.all_to_all(mod_cols, "shard", split_axis=0, concat_axis=1, tiled=True) + b_ada
    shift1, scale1, gate1, shift2, scale2, gate2 = [
        mod[:, i * width : (i + 1) * width] for i in range(6)
    ]
    tokens = latents[0].astype(jnp.float32)
    n_one, r_one = normalize(tokens)
    a_one = (n_one * (1.0 + scale1) + shift1).astype(jnp.bfloat16)
    grad_out = cotangent[0].astype(jnp.float32)
    d_mlp = grad_out * gate2
    d_mlp_b = d_mlp.astype(jnp.bfloat16)
    a_one2 = jnp.concatenate([a_one, swap(a_one)], axis=0)
    d_mlp2 = jnp.concatenate([d_mlp_b, swap(d_mlp_b)], axis=0)
    qkv = product("ld,de->le", a_one2, wq_b)
    shape = (2, length, heads, HD)
    queries = (qkv[:, :half] + b_q).astype(jnp.bfloat16).reshape(shape)
    key_rows = qkv[:, half : 2 * half].astype(jnp.bfloat16).reshape(shape)
    value_rows = (qkv[:, 2 * half :] + b_v).astype(jnp.bfloat16).reshape(shape)
    factor = HD ** (-0.5)
    scores = product("bqhd,bkhd->bhqk", queries, key_rows) * factor
    top = jnp.max(scores, axis=-1, keepdims=True)
    expo = jnp.exp(scores - top)
    probs = expo / jnp.sum(expo, axis=-1, keepdims=True)
    probs_b = probs.astype(jnp.bfloat16)
    heads_out = product("bhqk,bkhd->bqhd", probs_b, value_rows).astype(jnp.bfloat16)
    heads_flat = heads_out.reshape(2, length, half)
    heads_other = swap(heads_flat)[::-1]
    heads_own = ordered(heads_flat[0], heads_other[0], 1)
    attn = product("le,ed->ld", heads_own, wp_b) + b_proj
    x_one = tokens + gate1 * attn
    n_two, r_two = normalize(x_one)
    a_two = (n_two * (1.0 + scale2) + shift2).astype(jnp.bfloat16)
    a_two2 = jnp.concatenate([a_two, swap(a_two)], axis=0)
    mlp_sum = 0.0
    d_a2_sum = 0.0
    g_one = []
    g_two = []
    g_b_one = []
    for f in range(folds):
        pre = product("ld,df->lf", a_two2, w1_b[f]) + b_one[f]
        act_val, act_slope = gelu_parts(pre)
        act = act_val.astype(jnp.bfloat16)
        mlp_sum = mlp_sum + product("lf,fd->ld", act, w2_b[f])
        d_pre = product("ld,fd->lf", d_mlp2, w2_b[f]) * act_slope
        d_pre_b = d_pre.astype(jnp.bfloat16)
        d_a2_sum = d_a2_sum + product("lf,df->ld", d_pre_b, w1_b[f])
        g_one.append(product("ld,lf->df", a_two2, d_pre_b).astype(jnp.bfloat16))
        g_two.append(product("lf,ld->fd", act, d_mlp2).astype(jnp.bfloat16))
        g_b_one.append(jnp.sum(d_pre, axis=0))
    grads_mlp = lax.psum_scatter(
        jnp.concatenate(g_one + g_two, axis=1), "shard", scatter_dimension=0, tiled=True
    )
    d_a2 = d_a2_sum[:length] + swap(d_a2_sum[length:].astype(jnp.bfloat16)).astype(jnp.float32)
    mlp = mlp_sum[:length] + swap(mlp_sum[length:].astype(jnp.bfloat16)).astype(jnp.float32) + b_fc2
    block_out = (x_one + gate2 * mlp)[None]
    d_gate2 = jnp.sum(grad_out * mlp, axis=0)
    g_b_fc2 = jnp.sum(d_mlp, axis=0)
    d_shift2 = jnp.sum(d_a2, axis=0)
    d_scale2 = jnp.sum(d_a2 * n_two, axis=0)
    dx_one = grad_out + norm_back(d_a2 * (1.0 + scale2), n_two, r_two)
    d_gate1 = jnp.sum(dx_one * attn, axis=0)
    d_attn = dx_one * gate1
    d_attn_b = d_attn.astype(jnp.bfloat16)
    g_b_proj = jnp.sum(d_attn, axis=0)
    d_attn2 = jnp.concatenate([d_attn_b, swap(d_attn_b)], axis=0)
    d_heads = product("ld,ed->le", d_attn2, own_half(wp_b, 0)).astype(jnp.bfloat16).reshape(shape)
    heads_all = jnp.concatenate([heads_own, ordered(heads_flat[1], heads_other[1], 1)], axis=0)
    g_proj = product("le,ld->ed", heads_all, own_half(d_attn2, 1)).astype(jnp.bfloat16)
    delta = jnp.sum(d_heads.astype(jnp.float32) * heads_out.astype(jnp.float32), axis=-1)
    delta = jnp.transpose(delta, (0, 2, 1))[..., None]
    d_probs = product("bqhd,bkhd->bhqk", d_heads, value_rows)
    d_scores = (probs * (d_probs - delta) * factor).astype(jnp.bfloat16)
    d_q = product("bhqk,bkhd->bqhd", d_scores, key_rows)
    d_k = product("bhqk,bqhd->bkhd", d_scores, queries)
    d_v = product("bhqk,bqhd->bkhd", probs_b, d_heads)
    g_b_q = jnp.sum(d_q, axis=(0, 1)).reshape(half)
    g_b_v = jnp.sum(d_v, axis=(0, 1)).reshape(half)
    d_qkv = jnp.concatenate(
        [piece.astype(jnp.bfloat16).reshape(2 * length, half) for piece in (d_q, d_k, d_v)], axis=1
    )
    g_qkv = product("ld,le->de", a_one2, d_qkv).astype(jnp.bfloat16)
    grads_attn = lax.psum_scatter(
        jnp.concatenate([g_proj, g_qkv], axis=1), "shard", scatter_dimension=0, tiled=True
    )
    d_a1_sum = product("le,de->ld", d_qkv, wq_b)
    d_a1 = d_a1_sum[:length] + swap(d_a1_sum[length:].astype(jnp.bfloat16)).astype(jnp.float32)
    d_shift1 = jnp.sum(d_a1, axis=0)
    d_scale1 = jnp.sum(d_a1 * n_one, axis=0)
    latents_grad = (dx_one + norm_back(d_a1 * (1.0 + scale1), n_one, r_one))[None]
    d_mod = jnp.concatenate([d_shift1, d_scale1, d_gate1, d_shift2, d_scale2, d_gate2])
    d_mod_b = d_mod.astype(jnp.bfloat16).reshape(1, parts, d_mod.shape[0] // parts)
    d_mod_b = jnp.broadcast_to(d_mod_b, (replicas,) + d_mod_b.shape[1:])
    d_mod_cols = lax.all_to_all(
        d_mod_b.reshape(devices, d_mod_b.shape[2]), axes, split_axis=0, concat_axis=0, tiled=True
    )
    g_ada = jnp.dot(silu_all.T, d_mod_cols, preferred_element_type=jnp.float32)
    group_cols = lax.dynamic_slice_in_dim(d_mod_cols, rank * parts, parts, 0)
    silu_terms = jnp.dot(group_cols, ada_local.T, preferred_element_type=jnp.float32)
    silu_terms = lax.all_to_all(silu_terms, "shard", split_axis=0, concat_axis=0, tiled=True)
    silu_grad = jnp.sum(silu_terms, axis=0, keepdims=True)
    sig = jax.nn.sigmoid(cvec)
    cond_grad = silu_grad * sig * (1.0 + cvec * (1.0 - sig))
    mine = jnp.arange(2) == turn
    units_one = jnp.transpose(jnp.stack(g_b_one).reshape(folds, parts, unit), (1, 0, 2))
    bias_partial = jnp.concatenate(
        [
            jnp.where(mine[:, None], g_b_q[None], 0.0).reshape(inner),
            jnp.where(mine[:, None], g_b_v[None], 0.0).reshape(inner),
            g_b_proj,
            jnp.where(mine[None, :, None, None], units_one[:, None], 0.0).reshape(FF),
            g_b_fc2,
            d_mod,
        ]
    )
    chunk = bias_partial.shape[0] // devices
    bias_terms = lax.all_to_all(
        bias_partial.reshape(devices, chunk), axes, split_axis=0, concat_axis=0, tiled=True
    )
    bias_chunk = jnp.sum(bias_terms, axis=0)

    def complete(own):
        return swap(own) if replicas == 2 else jnp.zeros_like(own)

    def share(own, axis):
        if replicas == 2:
            return own
        return lax.psum_scatter(own.astype(jnp.float32), "rep", scatter_dimension=axis, tiled=True)

    def split(value):
        if replicas == 2:
            return own_half(value, 1)
        return share(value, 1)

    own_proj = grads_attn[:, :half]
    if replicas > 2:
        own_proj = share(ordered(own_proj, jnp.zeros_like(own_proj), 1), 1)
    own_qkv = grads_attn[:, half:].reshape(rows, 3, half)
    full_qkv = ordered(own_qkv, complete(own_qkv), 2).reshape(rows, 3 * inner)
    own_mlp = grads_mlp[:, None]
    full_mlp_grad = ordered(own_mlp, complete(own_mlp), 1)
    full_one = full_mlp_grad[:, :, : folds * width].reshape(rows, 2, folds, parts, unit)
    full_one = jnp.transpose(full_one, (0, 3, 1, 2, 4)).reshape(rows, FF)
    full_two = full_mlp_grad[:, :, folds * width :].reshape(rows, 2, folds, width)
    full_two = jnp.transpose(full_two, (1, 2, 0, 3)).reshape(2 * folds * rows, width)
    count_ada = width // replicas
    own_ada = lax.dynamic_slice_in_dim(g_ada, rank * count_ada, count_ada, 0)
    pieces = [split(full_qkv), own_proj, split(full_one), split(full_two), own_ada]
    pieces = [piece.astype(jnp.float32) for piece in pieces]
    if replicas == 2:
        counted = [grads_attn.astype(jnp.float32), grads_mlp.astype(jnp.float32), own_ada]
    else:
        counted = pieces
    squares = sum((jnp.sum(p * p) for p in counted)) + jnp.sum(bias_chunk * bias_chunk)
    totals = spread(jnp.concatenate([bias_chunk, squares[None]])[None])
    g_bias = totals[:, :chunk].reshape(devices * chunk)
    gnorm = jnp.sqrt(jnp.sum(totals[:, chunk]))
    clip = 1.0 / jnp.maximum(gnorm, 1.0)
    weights = (w_qkv, w_proj, w_fc1, w_fc2, w_ada)
    dims = (1, 1, 1, 1, 0)
    firsts = (m_qkv, m_proj, m_fc1, m_fc2, m_ada)
    seconds = (v_qkv, v_proj, v_fc1, v_fc2, v_ada)
    new_w = []
    new_m = []
    new_v = []
    for weight, dim, grad, first, second in zip(weights, dims, pieces, firsts, seconds):
        count = weight.shape[dim] // replicas
        own = lax.dynamic_slice_in_dim(weight, rank * count, count, dim)
        change, first_new, second_new = adam_change(own, grad, first, second, clip)
        change = change.astype(jnp.bfloat16)
        if replicas == 2:
            changes = ordered(change, swap(change), dim)
        else:
            changes = lax.all_gather(change, "rep", axis=dim, tiled=True)
        new_w.append(weight + changes.astype(jnp.float32))
        new_m.append(first_new)
        new_v.append(second_new)
    bias_update, new_m_bias, new_v_bias = adam_change(biases, g_bias, m_bias, v_bias, clip)
    return (
        block_out,
        latents_grad,
        cond_grad,
        *new_w,
        bias_update,
        *new_m,
        new_m_bias,
        *new_v,
        new_v_bias,
    )


def solution(mesh):
    in_specs = (
        P(("rep", "shard"), None, None),
        P(("rep", "shard"), None),
        P(("rep", "shard")),
        P(("rep", "shard"), None, None),
        P("shard", None),
        P("shard", None),
        P("shard", None),
        P("shard", None),
        P(None, "shard"),
        P(),
        P("shard", "rep"),
        P("shard", "rep"),
        P("shard", "rep"),
        P("shard", "rep"),
        P("rep", "shard"),
        P(),
        P("shard", "rep"),
        P("shard", "rep"),
        P("shard", "rep"),
        P("shard", "rep"),
        P("rep", "shard"),
        P(),
    )
    out_specs = (
        P(("rep", "shard"), None, None),
        P(("rep", "shard"), None, None),
        P(("rep", "shard"), None),
        P("shard", None),
        P("shard", None),
        P("shard", None),
        P("shard", None),
        P(None, "shard"),
        P(),
        P("shard", "rep"),
        P("shard", "rep"),
        P("shard", "rep"),
        P("shard", "rep"),
        P("rep", "shard"),
        P(),
        P("shard", "rep"),
        P("shard", "rep"),
        P("shard", "rep"),
        P("shard", "rep"),
        P("rep", "shard"),
        P(),
    )
    return jax.shard_map(shards, mesh=mesh, in_specs=in_specs, out_specs=out_specs, check_vma=False)
```

profile of v0, /device:TPU:0, one launch (start us, length us, event | category | flops | bytes accessed | tf_op | source)
XLA Modules:
  0.0 525.0 jit_solution(11382499632518451920)
XLA Ops:
  10.5 2.6 reshape.278
  20.7 7.3 %all-to-all-start = ((bf16[32,2,576]{2,1,0:T(2,128)(2,1)}), bf16[32,2,576]{2,1,0:T(2,128)(2,1)S(1)}, u32[]{:S(2)}, u32[]{:S(2)}) async-start(bf16[32,2,576]{2,1,0:T(2,128)(2,1)} %reshape.315), calls=%async_computation | async-start | bytes 163840 | tf_op jit(solution)/shard_map/all_to_all | solution.py:119
  28.5 8.4 %all-to-all-done = bf16[32,2,576]{2,1,0:T(2,128)(2,1)S(1)} async-done(((bf16[32,2,576]{2,1,0:T(2,128)(2,1)}), bf16[32,2,576]{2,1,0:T(2,128)(2,1)S(1)}, u32[]{:S(2)}, u32[]{:S(2)}) %all-to-all-start) | async-done | bytes 73760 | tf_op jit(solution)/shard_map/all_to_all | solution.py:119
  38.2 3.7 all-to-all-start.1
  42.3 6.2 %all-to-all-done.1 = f32[16,1,432]{2,1,0:T(1,128)S(1)} async-done(((f32[16,1,432]{2,1,0:T(1,128)}), f32[16,1,432]{2,1,0:T(1,128)S(1)}, u32[]{:S(2)}, u32[]{:S(2)}) %all-to-all-start.1) | async-done | bytes 27680 | tf_op jit(solution)/shard_map/all_to_all | solution.py:151
  50.1 7.9 %collective-permute-done = bf16[128,1152]{1,0:T(8,128)(2,1)S(1)} collective-permute-done((bf16[128,1152]{1,0:T(8,128)(2,1)S(1)}, bf16[128,1152]{1,0:T(8,128)(2,1)S(1)}, u32[]{:S(2)}, u32[]{:S(2)}) %collective-permute-start) | collective-permute-done | bytes 294944 | tf_op jit(solution)/shard_map/ppermute | solution.py:106
  57.9 21.5 %all-gather.3.cloned.1.call-done = bf16[1152,2880]{1,0:T(8,128)(2,1)} async-done(((bf16[72,2880]{1,0:T(8,128)(2,1)}), bf16[1152,2880]{1,0:T(8,128)(2,1)}) %all-gather.3.cloned.1.call-update) | async-done | bytes 6635536 | tf_op jit(solution)/shard_map/all_gather | solution.py:133
  79.4 4.0 fusion.3
  85.5 1.6 convolution_convert_fusion.7
  89.5 6.8 %collective-permute-done.1 = bf16[2,128,576]{1,2,0:T(8,128)(2,1)S(1)} collective-permute-done((bf16[2,128,576]{1,2,0:T(8,128)(2,1)S(1)}, bf16[2,128,576]{1,2,0:T(8,128)(2,1)S(1)}, u32[]{:S(2)}, u32[]{:S(2)}) %collective-permute-start.1) | collective-permute-done | bytes 294944 | tf_op jit(solution)/shard_map/ppermute | solution.py:106
  97.1 3.3 fusion.121
  103.7 7.1 %collective-permute-done.2 = bf16[128,1152]{1,0:T(8,128)(2,1)S(1)} collective-permute-done((bf16[128,1152]{1,0:T(8,128)(2,1)S(1)}, bf16[128,1152]{1,0:T(8,128)(2,1)S(1)}, u32[]{:S(2)}, u32[]{:S(2)}) %collective-permute-start.2) | collective-permute-done | bytes 294944 | tf_op jit(solution)/shard_map/ppermute | solution.py:106
  110.8 58.5 %all-gather.5.cloned.1.call-done = bf16[1152,4608]{1,0:T(8,128)(2,1)} async-done(((bf16[72,4608]{1,0:T(8,128)(2,1)}), bf16[1152,4608]{1,0:T(8,128)(2,1)}) %all-gather.5.cloned.1.call-update) | async-done | bytes 10616848 | tf_op jit(solution)/shard_map/all_gather | solution.py:142
  169.3 2.9 convolution_add_fusion.3
  172.3 3.9 convolution_add_fusion.2
  176.2 2.7 fusion.135
  180.7 2.8 fusion.134
  189.4 5.2 collective-permute-done.5
  195.4 4.7 collective-permute-done.3
  200.2 2.0 fusion.46
  204.6 6.0 %collective-permute-done.6 = bf16[128,1152]{1,0:T(8,128)(2,1)S(1)} collective-permute-done((bf16[128,1152]{1,0:T(8,128)(2,1)S(1)}, bf16[128,1152]{1,0:T(8,128)(2,1)S(1)}, u32[]{:S(2)}, u32[]{:S(2)}) %collective-permute-start.6) | collective-permute-done | bytes 294944 | tf_op jit(solution)/shard_map/ppermute | solution.py:106
  213.8 1.7 fusion.21
  221.4 2.7 pad_maximum_fusion.1
  224.1 8.6 %copy.290 = bf16[1152,2304]{1,0:T(8,128)(2,1)} copy(bf16[1152,2304]{0,1:T(8,128)(2,1)} %pad_maximum_fusion.1) | data formatting | bytes 10616832
  233.7 2.1 convolution_convert_fusion.2
  237.1 2.3 convolution_convert_fusion
  239.5 2.2 convolution_convert_fusion.1
  241.7 28.2 %pad_maximum_fusion = bf16[1152,4608]{0,1:T(8,128)(2,1)} fusion(bf16[1152,1152]{0,1:T(8,128)(2,1)S(1)} %convolution_convert_fusion, bf16[1152,1152]{0,1:T(8,128)(2,1)S(1)} %convolution_convert_fusion.1, bf16[1152,1152]{0,1:T(8,128)(2,1)S(1)} %convolution_convert_fusion.2, bf16[1152,1152]{0,1:T(8,128)(2,1)S(1)} %convolution_convert_fusion.3), kind=kLoop, calls=%fused_computation.1 | loop fusion | flops 42467328 | bytes 21233664 | tf_op jit(solution)/shard_map/concatenate | solution.py:200
  269.8 15.4 %copy.292 = bf16[1152,4608]{1,0:T(8,128)(2,1)} copy(bf16[1152,4608]{0,1:T(8,128)(2,1)} %pad_maximum_fusion) | data formatting | bytes 21233664
  288.1 1.8 copy.274
  290.6 4.0 fusion.1
  311.0 2.6 all-to-all-start.2
  313.6 2.2 fusion.55
  316.6 4.3 all-to-all-done.2
  320.8 2.6 all-to-all-start.4
  324.5 6.3 %all-to-all-done.4 = f32[32,1,504]{2,1,0:T(1,128)S(1)} async-done(((f32[32,1,504]{2,1,0:T(1,128)}), f32[32,1,504]{2,1,0:T(1,128)S(1)}, u32[]{:S(2)}, u32[]{:S(2)}) %all-to-all-start.4) | async-done | bytes 64544 | tf_op jit(solution)/shard_map/all_to_all | solution.py:265
  330.8 3.5 all-to-all-start.3
  337.7 3.5 all-to-all-done.3
  345.3 87.4 %reduce-scatter.9.cloned.1.call-done = bf16[72,4608]{1,0:T(8,128)(2,1)} async-done(((bf16[1152,4608]{1,0:T(8,128)(2,1)}), bf16[72,4608]{1,0:T(8,128)(2,1)}) %reduce-scatter.9.cloned.1.call-update) | async-done | bytes 663568
  432.6 1.6 copy.293
  438.8 4.6 all-to-all-start.5
  443.4 2.1 maximum_select_fusion.2
  447.6 1.9 collective-permute-start.11
  453.7 3.1 multiply_convert_fusion.6
  457.5 1.9 multiply_convert_fusion.7
  460.8 3.9 multiply_convert_fusion.2
  465.3 1.6 mul.751
  466.9 1.6 add_multiply_fusion
  468.5 1.8 copy.283
  471.1 3.3 collective-permute-done.10
  474.4 2.2 convert_add_fusion.5
  476.6 2.0 copy.282
  478.6 2.7 convert_add_fusion.3
  481.3 2.3 copy.278
  483.6 2.9 maximum_select_fusion
  487.7 2.3 copy.280
  489.9 5.0 reshape.287
  495.0 2.9 multiply_convert_fusion.4
  497.8 1.9 collective-permute-start.12
  499.7 3.5 convert_add_fusion
  503.3 1.7 copy.281
  505.0 3.2 multiply_convert_fusion.3
  508.3 2.6 convert_add_fusion.2
  510.9 5.9 %collective-permute-done.13 = bf16[288,576]{1,0:T(8,128)(2,1)S(1)} collective-permute-done((bf16[288,576]{1,0:T(8,128)(2,1)S(1)}, bf16[288,576]{1,0:T(8,128)(2,1)S(1)}, u32[]{:S(2)}, u32[]{:S(2)}) %collective-permute-start.13) | collective-permute-done | bytes 331808 | tf_op jit(solution)/shard_map/ppermute | solution.py:106
  (316 shorter events, 86.7 us)
Async XLA Ops:
  7.2 72.2 %all-gather.3.cloned.1.call-start = ((), (), s32[]{:S(2)}) async-start(), calls=%async_computation.8 | async-start | bytes 7206912 | tf_op jit(solution)/shard_map/all_gather | solution.py:133
  10.3 159.0 %all-gather.5.cloned.1.call-start = ((), (), s32[]{:S(2)}) async-start(), calls=%async_computation.9 | async-start | bytes 11280384 | tf_op jit(solution)/shard_map/all_gather | solution.py:142
  15.6 1.9 copy-start.56
  15.7 12.4 %copy-start.1 = (bf16[1,128,1152]{2,1,0:T(8,128)(2,1)S(1)}, bf16[1,128,1152]{2,1,0:T(8,128)(2,1)}, u32[]{:S(2)}) copy-start(bf16[1,128,1152]{2,1,0:T(8,128)(2,1)} %param.22) | copy-start | bytes 884740
  16.6 20.6 %copy-start = (f32[1152,432]{0,1:T(8,128)S(1)}, f32[1152,432]{0,1:T(8,128)}, u32[]{:S(2)}) copy-start(f32[1152,432]{0,1:T(8,128)} %param.30) | copy-start | bytes 5971972
  20.7 16.2 %all-to-all-start = ((bf16[32,2,576]{2,1,0:T(2,128)(2,1)}), bf16[32,2,576]{2,1,0:T(2,128)(2,1)S(1)}, u32[]{:S(2)}, u32[]{:S(2)}) async-start(bf16[32,2,576]{2,1,0:T(2,128)(2,1)} %reshape.315), calls=%async_computation | async-start | bytes 163840 | tf_op jit(solution)/shard_map/all_to_all | solution.py:119
  28.2 20.7 %copy-start.55 = (f32[128]{0:T(128)}, f32[128]{0:T(128)S(1)}, u32[]{:S(2)}) copy-start(f32[128]{0:T(128)S(1)} %broadcast_multiply_fusion.5) | copy-start | bytes 1540
  37.1 5.2 copy-start.35
  37.1 5.1 copy-start.41
  38.2 10.4 %all-to-all-start.1 = ((f32[16,1,432]{2,1,0:T(1,128)}), f32[16,1,432]{2,1,0:T(1,128)S(1)}, u32[]{:S(2)}, u32[]{:S(2)}) async-start(f32[16,1,432]{2,1,0:T(1,128)} %copy.246), calls=%async_computation.1 | async-start | bytes 65536 | tf_op jit(solution)/shard_map/all_to_all | solution.py:151
  41.9 300.0 %reduce-scatter.7.cloned.1.call-start = ((), (), s32[]{:S(2)}) async-start(), calls=%async_computation.10 | async-start | bytes 5640192
  42.2 7.0 %copy-start.57 = (f32[128]{0:T(128)}, f32[128]{0:T(128)S(1)}, u32[]{:S(2)}) copy-start(f32[128]{0:T(128)S(1)} %add_rsqrt_fusion.1) | copy-start | bytes 1540
  49.2 34.3 %copy-start.19 = (bf16[128,1152]{1,0:T(8,128)(2,1)}, bf16[128,1152]{1,0:T(8,128)(2,1)S(1)}, u32[]{:S(2)}) copy-start(bf16[128,1152]{1,0:T(8,128)(2,1)S(1)} %fusion.50) | copy-start | bytes 884740
  49.2 8.8 %collective-permute-start = (bf16[128,1152]{1,0:T(8,128)(2,1)S(1)}, bf16[128,1152]{1,0:T(8,128)(2,1)S(1)}, u32[]{:S(2)}, u32[]{:S(2)}) collective-permute-start(bf16[128,1152]{1,0:T(8,128)(2,1)S(1)} %fusion.50), channel_id=1, source_target_pairs={{0,16},{16,0},{1,17},{17,1},{2,18},{18,2},{3,19},{19,3},{4,20},{20... | collective-permute-start | bytes 884744 | tf_op jit(solution)/shard_map/ppermute | solution.py:106
  57.9 21.5 %copy-start.43 = (bf16[128,1152]{1,0:T(8,128)(2,1)}, bf16[128,1152]{1,0:T(8,128)(2,1)S(1)}, u32[]{:S(2)}) copy-start(bf16[128,1152]{1,0:T(8,128)(2,1)S(1)} %collective-permute-done) | copy-start | bytes 884740
  84.0 3.1 copy-start.27
  87.1 10.0 %copy-start.23 = (bf16[2,8,72,128]{3,2,1,0:T(8,128)(2,1)}, bf16[2,8,72,128]{3,2,1,0:T(8,128)(2,1)S(1)}, u32[]{:S(2)}) copy-start(bf16[2,8,72,128]{3,2,1,0:T(8,128)(2,1)S(1)} %convolution_convert_fusion.7) | copy-start | bytes 884740
  87.1 9.2 %collective-permute-start.1 = (bf16[2,128,576]{1,2,0:T(8,128)(2,1)S(1)}, bf16[2,128,576]{1,2,0:T(8,128)(2,1)S(1)}, u32[]{:S(2)}, u32[]{:S(2)}) collective-permute-start(bf16[2,128,576]{1,2,0:T(8,128)(2,1)S(1)} %bitcast.156), channel_id=1, source_target_pairs={{0,16},{16,0},{1,17},{17,1},{2,18},{18,2},{3,19},{19,3},{4,20},{20... | collective-permute-start | bytes 884744 | tf_op jit(solution)/shard_map/ppermute | solution.py:106
  97.1 3.4 copy-start.21
  100.4 2.0 copy-start.17
  100.8 71.4 %copy-start.10 = (bf16[128,1152]{1,0:T(8,128)(2,1)}, bf16[128,1152]{1,0:T(8,128)(2,1)S(1)}, u32[]{:S(2)}) copy-start(bf16[128,1152]{1,0:T(8,128)(2,1)S(1)} %add_convert_fusion) | copy-start | bytes 884740
  100.8 9.9 %collective-permute-start.2 = (bf16[128,1152]{1,0:T(8,128)(2,1)S(1)}, bf16[128,1152]{1,0:T(8,128)(2,1)S(1)}, u32[]{:S(2)}, u32[]{:S(2)}) collective-permute-start(bf16[128,1152]{1,0:T(8,128)(2,1)S(1)} %add_convert_fusion), channel_id=1, source_target_pairs={{0,16},{16,0},{1,17},{17,1},{2,18},{18,2},{3,19},{19,3},{4,20},{20... | collective-permute-start | bytes 884744 | tf_op jit(solution)/shard_map/ppermute | solution.py:106
  103.1 73.0 %collective-permute-start.4 = (bf16[128,1152]{1,0:T(8,128)(2,1)}, bf16[128,1152]{1,0:T(8,128)(2,1)}, u32[]{:S(2)}, u32[]{:S(2)}) collective-permute-start(bf16[128,1152]{1,0:T(8,128)(2,1)} %fusion.47), channel_id=1, source_target_pairs={{0,16},{16,0},{1,17},{17,1},{2,18},{18,2},{3,19},{19,3},{4,20},{20... | collective-permute-start | bytes 884744 | tf_op jit(solution)/shard_map/ppermute | solution.py:106
  110.8 61.5 %copy-start.31 = (bf16[128,1152]{1,0:T(8,128)(2,1)}, bf16[128,1152]{1,0:T(8,128)(2,1)S(1)}, u32[]{:S(2)}) copy-start(bf16[128,1152]{1,0:T(8,128)(2,1)S(1)} %collective-permute-done.2) | copy-start | bytes 884740
  169.3 6.8 %copy-start.34 = (bf16[1152,4608]{1,0:T(8,128)(2,1)S(1)}, bf16[1152,4608]{1,0:T(8,128)(2,1)}, u32[]{:S(2)}) copy-start(bf16[1152,4608]{1,0:T(8,128)(2,1)} %all-gather.5.cloned.1.call-done) | copy-start | bytes 31850500
  172.3 13.9 %copy-start.62 = (f32[256,1152]{1,0:T(8,128)}, f32[256,1152]{1,0:T(8,128)S(1)}, u32[]{:S(2)}) copy-start(f32[256,1152]{1,0:T(8,128)S(1)} %convolution_add_fusion.3) | copy-start | bytes 3538948
  176.2 11.1 %copy-start.64 = (f32[256,1152]{1,0:T(8,128)}, f32[256,1152]{1,0:T(8,128)S(1)}, u32[]{:S(2)}) copy-start(f32[256,1152]{1,0:T(8,128)S(1)} %convolution_add_fusion.2) | copy-start | bytes 3538948
  184.6 9.9 %collective-permute-start.5 = (bf16[128,1152]{1,0:T(8,128)(2,1)S(1)}, bf16[128,1152]{1,0:T(8,128)(2,1)S(1)}, u32[]{:S(2)}, u32[]{:S(2)}) collective-permute-start(bf16[128,1152]{1,0:T(8,128)(2,1)S(1)} %slice.300), channel_id=1, source_target_pairs={{0,16},{16,0},{1,17},{17,1},{2,18},{18,2},{3,19},{19,3},{4,20},{20... | collective-permute-start | bytes 884744 | tf_op jit(solution)/shard_map/ppermute | solution.py:106
  188.7 11.4 %copy-start.12 = (f32[128,1152]{1,0:T(8,128)S(1)}, f32[128,1152]{1,0:T(8,128)}, u32[]{:S(2)}) copy-start(f32[128,1152]{1,0:T(8,128)} %get-tuple-element.250) | copy-start | bytes 1769476
  188.8 11.4 %copy-start.18 = (bf16[1,128,1152]{2,1,0:T(8,128)(2,1)S(1)}, bf16[1,128,1152]{2,1,0:T(8,128)(2,1)}, u32[]{:S(2)}) copy-start(bf16[1,128,1152]{2,1,0:T(8,128)(2,1)} %param.25) | copy-start | bytes 884740
  188.8 11.4 %collective-permute-start.3 = (bf16[128,1152]{1,0:T(8,128)(2,1)S(1)}, bf16[128,1152]{1,0:T(8,128)(2,1)S(1)}, u32[]{:S(2)}, u32[]{:S(2)}) collective-permute-start(bf16[128,1152]{1,0:T(8,128)(2,1)S(1)} %slice.301), channel_id=1, source_target_pairs={{0,16},{16,0},{1,17},{17,1},{2,18},{18,2},{3,19},{19,3},{4,20},{20... | collective-permute-start | bytes 884744 | tf_op jit(solution)/shard_map/ppermute | solution.py:106
  202.2 8.4 %copy-start.45 = (bf16[128,1152]{1,0:T(8,128)(2,1)}, bf16[128,1152]{1,0:T(8,128)(2,1)S(1)}, u32[]{:S(2)}) copy-start(bf16[128,1152]{1,0:T(8,128)(2,1)S(1)} %multiply_convert_fusion.5) | copy-start | bytes 884740
  202.2 9.1 %slice-start = ((bf16[1152,2880]{1,0:T(8,128)(2,1)}), bf16[1152,1152]{1,0:T(8,128)(2,1)S(1)}, s32[]{:S(2)}) async-start(bf16[1152,2880]{1,0:T(8,128)(2,1)} %all-gather.3.cloned.1.call-done), calls=%async_computation.12 | async-start | bytes 5308416 | tf_op jit(solution)/shard_map/slice | solution.py:134
  202.2 8.4 %collective-permute-start.6 = (bf16[128,1152]{1,0:T(8,128)(2,1)S(1)}, bf16[128,1152]{1,0:T(8,128)(2,1)S(1)}, u32[]{:S(2)}, u32[]{:S(2)}) collective-permute-start(bf16[128,1152]{1,0:T(8,128)(2,1)S(1)} %multiply_convert_fusion.5), channel_id=1, source_target_pairs={{0,16},{16,0},{1,17},{17,1},{2,18},{18,2},{3,19},{19,3},{4,20},{20... | collective-permute-start | bytes 884744 | tf_op jit(solution)/shard_map/ppermute | solution.py:106
  204.6 9.1 %copy-start.24 = (bf16[2,8,72,128]{3,2,1,0:T(8,128)(2,1)S(1)}, bf16[2,8,72,128]{3,2,1,0:T(8,128)(2,1)}, u32[]{:S(2)}) copy-start(bf16[2,8,72,128]{3,2,1,0:T(8,128)(2,1)} %copy-done.23) | copy-start | bytes 884740
  213.8 1.8 copy-start.26
  232.7 200.0 %reduce-scatter.9.cloned.1.call-start = ((), (), s32[]{:S(2)}) async-start(), calls=%async_computation.11 | async-start | bytes 11280384
  233.7 2.1 copy-start.40
  237.1 2.3 copy-start.63
  285.2 2.0 copy-start.49
  285.2 4.7 copy-start.54
  295.7 9.2 %collective-permute-start.7 = (bf16[128,1152]{1,0:T(8,128)(2,1)S(1)}, bf16[128,1152]{1,0:T(8,128)(2,1)S(1)}, u32[]{:S(2)}, u32[]{:S(2)}) collective-permute-start(bf16[128,1152]{1,0:T(8,128)(2,1)S(1)} %slice.299), channel_id=1, source_target_pairs={{0,16},{16,0},{1,17},{17,1},{2,18},{18,2},{3,19},{19,3},{4,20},{20... | collective-permute-start | bytes 884744 | tf_op jit(solution)/shard_map/ppermute | solution.py:106
  311.0 9.8 %all-to-all-start.2 = ((bf16[32,2,216]{2,1,0:T(2,128)(2,1)}), bf16[32,2,216]{2,1,0:T(2,128)(2,1)S(1)}, u32[]{:S(2)}, u32[]{:S(2)}) async-start(bf16[32,2,216]{2,1,0:T(2,128)(2,1)} %reshape.317), calls=%async_computation.2 | async-start | bytes 65536 | tf_op jit(solution)/shard_map/all_to_all | solution.py:242
  320.8 10.0 %all-to-all-start.4 = ((f32[32,1,504]{2,1,0:T(1,128)}), f32[32,1,504]{2,1,0:T(1,128)S(1)}, u32[]{:S(2)}, u32[]{:S(2)}) async-start(f32[32,1,504]{2,1,0:T(1,128)} %all_to_all.52), calls=%async_computation.4 | async-start | bytes 131072 | tf_op jit(solution)/shard_map/all_to_all | solution.py:265
  323.6 10.8 %copy-start.36 = (bf16[32,1,1152]{2,1,0:T(2,128)(2,1)S(1)}, bf16[32,1,1152]{2,1,0:T(2,128)(2,1)}, u32[]{:S(2)}) copy-start(bf16[32,1,1152]{2,1,0:T(2,128)(2,1)} %copy-done.35) | copy-start | bytes 221188
  330.8 10.5 %all-to-all-start.3 = ((f32[16,1,1152]{2,1,0:T(1,128)}), f32[16,1,1152]{2,1,0:T(1,128)S(1)}, u32[]{:S(2)}, u32[]{:S(2)}) async-start(f32[16,1,1152]{2,1,0:T(1,128)} %copy.267), calls=%async_computation.3 | async-start | bytes 147456 | tf_op jit(solution)/shard_map/all_to_all | solution.py:248
  334.4 7.0 %copy-start.51 = (f32[1,1152]{1,0:T(1,128)S(1)}, f32[1,1152]{1,0:T(1,128)}, u32[]{:S(2)}) copy-start(f32[1,1152]{1,0:T(1,128)} %get-tuple-element.210) | copy-start | bytes 13828
  334.4 7.0 %copy-start.52 = (f32[1,1152]{1,0:T(1,128)S(1)}, f32[1,1152]{1,0:T(1,128)}, u32[]{:S(2)}) copy-start(f32[1,1152]{1,0:T(1,128)} %get-tuple-element.211) | copy-start | bytes 13828
  343.3 2.0 copy-start.6
  343.6 99.8 %collective-permute-start.8 = (bf16[72,3,576]{2,1,0:T(4,128)(2,1)S(1)}, bf16[72,3,576]{2,1,0:T(4,128)(2,1)}, u32[]{:S(2)}, u32[]{:S(2)}) collective-permute-start(bf16[72,3,576]{2,1,0:T(4,128)(2,1)S(1)} %copy.269), channel_id=1, source_target_pairs={{0,16},{16,0},{1,17},{17,1},{2,18},{18,2},{3,19},{19,3},{4,20},{20... | collective-permute-start | bytes 746504 | tf_op jit(solution)/shard_map/ppermute | solution.py:106
  438.8 11.9 %all-to-all-start.5 = ((f32[32,1,505]{2,1,0:T(1,128)}), f32[32,1,505]{2,1,0:T(1,128)}, u32[]{:S(2)}, u32[]{:S(2)}) async-start(f32[32,1,505]{2,1,0:T(1,128)} %broadcast_in_dim.121), calls=%async_computation.5 | async-start | bytes 131072 | tf_op jit(solution)/shard_map/all_to_all | solution.py:119
  447.6 33.7 %collective-permute-start.11 = (bf16[72,1,4608]{2,0,1:T(8,128)(2,1)}, bf16[72,1,4608]{2,0,1:T(8,128)(2,1)}, u32[]{:S(2)}, u32[]{:S(2)}) collective-permute-start(bf16[72,1,4608]{2,0,1:T(8,128)(2,1)} %copy.277), channel_id=1, source_target_pairs={{0,16},{16,0},{1,17},{17,1},{2,18},{18,2},{3,19},{19,3},{4,20},{20... | collective-permute-start | bytes 1990664 | tf_op jit(solution)/shard_map/ppermute | solution.py:106
  453.0 4.5 copy-start.30
  453.7 3.8 copy-start.8
  453.7 3.8 copy-start.29
  453.7 7.1 %copy-start.3 = (f32[1152,432]{0,1:T(8,128)S(1)}, f32[1152,432]{0,1:T(8,128)}, u32[]{:S(2)}) copy-start(f32[1152,432]{0,1:T(8,128)} %copy-done.2) | copy-start | bytes 5971972
  456.8 3.9 copy-start.33
  456.8 21.8 %collective-permute-start.9 = (bf16[72,1728]{1,0:T(8,128)(2,1)}, bf16[72,1728]{1,0:T(8,128)(2,1)}, u32[]{:S(2)}, u32[]{:S(2)}) collective-permute-start(bf16[72,1728]{1,0:T(8,128)(2,1)} %get-tuple-element.203), channel_id=1, source_target_pairs={{0,16},{16,0},{1,17},{17,1},{2,18},{18,2},{3,19},{19,3},{4,20},{20... | collective-permute-start | bytes 746504 | tf_op jit(solution)/shard_map/ppermute | solution.py:106
  459.4 7.5 %copy-start.42 = (f32[16128]{0:T(1024)S(1)}, f32[16128]{0:T(1024)}, u32[]{:S(2)}) copy-start(f32[16128]{0:T(1024)} %param.31) | copy-start | bytes 193540
  459.4 15.0 %collective-permute-start.10 = (bf16[72,576]{0,1:T(8,128)(2,1)}, bf16[72,576]{0,1:T(8,128)(2,1)}, u32[]{:S(2)}, u32[]{:S(2)}) collective-permute-start(bf16[72,576]{0,1:T(8,128)(2,1)} %get-tuple-element.200), channel_id=1, source_target_pairs={{0,16},{16,0},{1,17},{17,1},{2,18},{18,2},{3,19},{19,3},{4,20},{20... | collective-permute-start | bytes 248840 | tf_op jit(solution)/shard_map/ppermute | solution.py:106
  464.6 35.1 %collective-permute-start.14 = (bf16[576,432]{0,1:T(8,128)(2,1)}, bf16[576,432]{0,1:T(8,128)(2,1)}, u32[]{:S(2)}, u32[]{:S(2)}) collective-permute-start(bf16[576,432]{0,1:T(8,128)(2,1)} %get-tuple-element.191), channel_id=1, source_target_pairs={{0,16},{16,0},{1,17},{17,1},{2,18},{18,2},{3,19},{19,3},{4,20},{20... | collective-permute-start | bytes 1493000 | tf_op jit(solution)/shard_map/ppermute | solution.py:106
  489.9 5.0 copy-start.5
  497.8 10.5 %collective-permute-start.12 = (bf16[72,2304]{1,0:T(8,128)(2,1)}, bf16[72,2304]{1,0:T(8,128)(2,1)}, u32[]{:S(2)}, u32[]{:S(2)}) collective-permute-start(bf16[72,2304]{1,0:T(8,128)(2,1)} %get-tuple-element.197), channel_id=1, source_target_pairs={{0,16},{16,0},{1,17},{17,1},{2,18},{18,2},{3,19},{19,3},{4,20},{20... | collective-permute-start | bytes 995336 | tf_op jit(solution)/shard_map/ppermute | solution.py:106
  508.2 8.6 %collective-permute-start.13 = (bf16[288,576]{1,0:T(8,128)(2,1)S(1)}, bf16[288,576]{1,0:T(8,128)(2,1)S(1)}, u32[]{:S(2)}, u32[]{:S(2)}) collective-permute-start(bf16[288,576]{1,0:T(8,128)(2,1)S(1)} %get-tuple-element.194), channel_id=1, source_target_pairs={{0,16},{16,0},{1,17},{17,1},{2,18},{18,2},{3,19},{19,3},{4,20},{20... | collective-permute-start | bytes 995336 | tf_op jit(solution)/shard_map/ppermute | solution.py:106
  (30 other events, 37.4 us)
Sparse Core Ops, SparseCore 0:
  10.7 68.6 all-gather.2
  82.3 87.0 all-gather.4
  232.8 76.2 reduce-scatter.6
  313.0 119.5 reduce-scatter.8
where the time goes:
time: 533 us; the launch traced here: 525 us
  waiting for transfers between devices  244 us (46%)
  other arithmetic  88.4 us (17%)
  local copies, waits for them, and re-layouts  84.7 us (16%)
  matrix products  46.5 us (9%)
  starting transfers between devices  41.5 us (8%)
  between operations  19.5 us (4%)
    unnamed x6, waiting for transfers between devices  87.4 us
    all_gather x1, waiting for transfers between devices, shards(): full_mlp = lax.all_gather(pack_mlp, 'shard', axis=0, tiled=True)  58.5 us
    unnamed x164, local copies, waits for them, and re-layouts  54.4 us
    ppermute x15, waiting for transfers between devices, swap(): return lax.ppermute(value, 'rep', couples)  46.9 us
    dot_general x23, matrix products, product(): return jnp.einsum(form, left, right, preferred_element_type=jnp.float32)  44 us
    concatenate x1, other arithmetic, shards(): jnp.concatenate(g_one + g_two, axis=1)  28.2 us
    all_gather x1, waiting for transfers between devices, shards(): full_attn = lax.all_gather(pack_attn, 'shard', axis=0, tiled=True)  21.5 us
    ppermute x15, starting transfers between devices, swap(): return lax.ppermute(value, 'rep', couples)  16.9 us
  transfers between devices with their start and end apart: 25, of which 17 were waited for; matrix products, arithmetic and copies ran while one was open for 34% of the time, Pallas kernels for 0%

commit v1 on v0

--- a/solution.py
+++ b/solution.py
@@ -148,7 +148,15 @@
     silu_all = spread(silu_c)
     silu_group = lax.dynamic_slice_in_dim(silu_all, rank * parts, parts, 0)
     mod_cols = jnp.dot(silu_group, ada_local, preferred_element_type=jnp.float32)
-    mod = lax.all_to_all(mod_cols, "shard", split_axis=0, concat_axis=1, tiled=True) + b_ada
+    mod = (
+        jnp.concatenate(
+            lax.all_to_all(
+                jnp.stack(jnp.split(mod_cols, lax.axis_size("shard"), axis=0)), "shard", 0, 0
+            ),
+            axis=1,
+        )
+        + b_ada
+    )
     shift1, scale1, gate1, shift2, scale2, gate2 = [
         mod[:, i * width : (i + 1) * width] for i in range(6)
     ]

time: 533 us -> 534 us (level)
  local copies, waits for them, and re-layouts: 84.7 us -> 93.3 us
  waiting for transfers between devices: 244 us -> 236 us
    unnamed x164 -> x179, local copies, waits for them, and re-layouts: 54.4 us -> 63.1 us
    all_gather x1, waiting for transfers between devices: 21.5 us -> 12.9 us  [shards(): full_attn = lax.all_gather(pack_attn, 'shard', axis=0, tiled=True)]
  transfers between devices with their start and end apart: 25 -> 25, of which waited for: 17 -> 17; matrix products, arithmetic and copies ran while one was open for 34% -> 35% of each run, Pallas kernels for 0% -> 0%
where the time goes in v1:
time: 534 us; the launch traced here: 526 us
  waiting for transfers between devices  236 us (44%)
  local copies, waits for them, and re-layouts  93.3 us (17%)
  other arithmetic  88.4 us (17%)
  matrix products  46.4 us (9%)
  starting transfers between devices  41.7 us (8%)
  between operations  19.5 us (4%)
    unnamed x6, waiting for transfers between devices  87.7 us
    unnamed x179, local copies, waits for them, and re-layouts  63.1 us
    all_gather x1, waiting for transfers between devices, shards(): full_mlp = lax.all_gather(pack_mlp, 'shard', axis=0, tiled=True)  58.6 us
    ppermute x15, waiting for transfers between devices, swap(): return lax.ppermute(value, 'rep', couples)  46.5 us
    dot_general x23, matrix products, product(): return jnp.einsum(form, left, right, preferred_element_type=jnp.float32)  43.9 us
    concatenate x1, other arithmetic, shards(): jnp.concatenate(g_one + g_two, axis=1)  28.2 us
    ppermute x15, starting transfers between devices, swap(): return lax.ppermute(value, 'rep', couples)  17.1 us
    convert_element_type x5, other arithmetic, shards(): change = change.astype(jnp.bfloat16)  15 us
  transfers between devices with their start and end apart: 25, of which 17 were waited for; matrix products, arithmetic and copies ran while one was open for 35% of the time, Pallas kernels for 0%

profile of v1, /device:TPU:0, one launch (start us, length us, event | category | flops | bytes accessed | tf_op | source)
XLA Modules:
  0.0 525.7 jit_solution(714546707629774295)
XLA Ops:
  10.5 2.6 reshape.276
  20.7 7.3 %all-to-all-start = ((bf16[32,2,576]{2,1,0:T(2,128)(2,1)}), bf16[32,2,576]{2,1,0:T(2,128)(2,1)S(1)}, u32[]{:S(2)}, u32[]{:S(2)}) async-start(bf16[32,2,576]{2,1,0:T(2,128)(2,1)} %reshape.313), calls=%async_computation | async-start | bytes 163840 | tf_op jit(solution)/shard_map/all_to_all | solution.py:119
  28.5 8.4 %all-to-all-done = bf16[32,2,576]{2,1,0:T(2,128)(2,1)S(1)} async-done(((bf16[32,2,576]{2,1,0:T(2,128)(2,1)}), bf16[32,2,576]{2,1,0:T(2,128)(2,1)S(1)}, u32[]{:S(2)}, u32[]{:S(2)}) %all-to-all-start) | async-done | bytes 73760 | tf_op jit(solution)/shard_map/all_to_all | solution.py:119
  46.9 3.7 all-to-all-start.1
  51.0 6.9 %all-to-all-done.1 = f32[16,1,432]{2,1,0:T(1,128)S(1)} async-done(((f32[16,1,432]{2,1,0:T(1,128)}), f32[16,1,432]{2,1,0:T(1,128)S(1)}, u32[]{:S(2)}, u32[]{:S(2)}) %all-to-all-start.1) | async-done | bytes 27680 | tf_op jit(solution)/shard_map/all_to_all | solution.py:153
  59.3 7.5 %collective-permute-done = bf16[128,1152]{1,0:T(8,128)(2,1)S(1)} collective-permute-done((bf16[128,1152]{1,0:T(8,128)(2,1)S(1)}, bf16[128,1152]{1,0:T(8,128)(2,1)S(1)}, u32[]{:S(2)}, u32[]{:S(2)}) %collective-permute-start) | collective-permute-done | bytes 294944 | tf_op jit(solution)/shard_map/ppermute | solution.py:106
  66.9 12.9 %all-gather.3.cloned.1.call-done = bf16[1152,2880]{1,0:T(8,128)(2,1)} async-done(((bf16[72,2880]{1,0:T(8,128)(2,1)}), bf16[1152,2880]{1,0:T(8,128)(2,1)}) %all-gather.3.cloned.1.call-update) | async-done | bytes 6635536 | tf_op jit(solution)/shard_map/all_gather | solution.py:133
  79.8 4.0 fusion.3
  89.8 6.8 %collective-permute-done.1 = bf16[2,128,576]{1,2,0:T(8,128)(2,1)S(1)} collective-permute-done((bf16[2,128,576]{1,2,0:T(8,128)(2,1)S(1)}, bf16[2,128,576]{1,2,0:T(8,128)(2,1)S(1)}, u32[]{:S(2)}, u32[]{:S(2)}) %collective-permute-start.1) | collective-permute-done | bytes 294944 | tf_op jit(solution)/shard_map/ppermute | solution.py:106
  97.4 3.3 fusion.122
  104.0 7.1 %collective-permute-done.2 = bf16[128,1152]{1,0:T(8,128)(2,1)S(1)} collective-permute-done((bf16[128,1152]{1,0:T(8,128)(2,1)S(1)}, bf16[128,1152]{1,0:T(8,128)(2,1)S(1)}, u32[]{:S(2)}, u32[]{:S(2)}) %collective-permute-start.2) | collective-permute-done | bytes 294944 | tf_op jit(solution)/shard_map/ppermute | solution.py:106
  111.1 58.6 %all-gather.5.cloned.1.call-done = bf16[1152,4608]{1,0:T(8,128)(2,1)} async-done(((bf16[72,4608]{1,0:T(8,128)(2,1)}), bf16[1152,4608]{1,0:T(8,128)(2,1)}) %all-gather.5.cloned.1.call-update) | async-done | bytes 10616848 | tf_op jit(solution)/shard_map/all_gather | solution.py:142
  169.7 2.9 convolution_add_fusion.3
  172.7 3.9 convolution_add_fusion.2
  176.6 2.7 fusion.136
  181.1 2.8 fusion.135
  189.8 5.1 collective-permute-done.5
  195.8 4.7 collective-permute-done.3
  200.6 2.0 fusion.46
  205.0 6.0 %collective-permute-done.6 = bf16[128,1152]{1,0:T(8,128)(2,1)S(1)} collective-permute-done((bf16[128,1152]{1,0:T(8,128)(2,1)S(1)}, bf16[128,1152]{1,0:T(8,128)(2,1)S(1)}, u32[]{:S(2)}, u32[]{:S(2)}) %collective-permute-start.6) | collective-permute-done | bytes 294944 | tf_op jit(solution)/shard_map/ppermute | solution.py:106
  214.2 1.7 fusion.21
  221.7 2.7 pad_maximum_fusion.1
  224.5 8.6 %copy.285 = bf16[1152,2304]{1,0:T(8,128)(2,1)} copy(bf16[1152,2304]{0,1:T(8,128)(2,1)} %pad_maximum_fusion.1) | data formatting | bytes 10616832
  234.1 2.1 convolution_convert_fusion.2
  237.5 2.3 convolution_convert_fusion
  239.9 2.2 convolution_convert_fusion.1
  242.0 28.2 %pad_maximum_fusion = bf16[1152,4608]{0,1:T(8,128)(2,1)} fusion(bf16[1152,1152]{0,1:T(8,128)(2,1)S(1)} %convolution_convert_fusion, bf16[1152,1152]{0,1:T(8,128)(2,1)S(1)} %convolution_convert_fusion.1, bf16[1152,1152]{0,1:T(8,128)(2,1)S(1)} %convolution_convert_fusion.2, bf16[1152,1152]{0,1:T(8,128)(2,1)S(1)} %convolution_convert_fusion.3), kind=kLoop, calls=%fused_computation.1 | loop fusion | flops 42467328 | bytes 21233664 | tf_op jit(solution)/shard_map/concatenate | solution.py:208
  270.2 15.3 %copy.287 = bf16[1152,4608]{1,0:T(8,128)(2,1)} copy(bf16[1152,4608]{0,1:T(8,128)(2,1)} %pad_maximum_fusion) | data formatting | bytes 21233664
  288.4 1.8 copy.269
  291.0 4.0 fusion.1
  296.0 1.7 collective-permute-start.7
  311.4 2.6 all-to-all-start.2
  314.0 2.2 fusion.55
  317.0 4.3 all-to-all-done.2
  321.2 2.6 all-to-all-start.4
  325.0 6.3 %all-to-all-done.4 = f32[32,1,504]{2,1,0:T(1,128)S(1)} async-done(((f32[32,1,504]{2,1,0:T(1,128)}), f32[32,1,504]{2,1,0:T(1,128)S(1)}, u32[]{:S(2)}, u32[]{:S(2)}) %all-to-all-start.4) | async-done | bytes 64544 | tf_op jit(solution)/shard_map/all_to_all | solution.py:273
  331.2 3.5 all-to-all-start.3
  338.1 3.5 all-to-all-done.3
  345.7 87.6 %reduce-scatter.9.cloned.1.call-done = bf16[72,4608]{1,0:T(8,128)(2,1)} async-done(((bf16[1152,4608]{1,0:T(8,128)(2,1)}), bf16[72,4608]{1,0:T(8,128)(2,1)}) %reduce-scatter.9.cloned.1.call-update) | async-done | bytes 663568
  433.3 1.6 copy.288
  439.5 4.6 all-to-all-start.5
  444.1 2.1 maximum_select_fusion.2
  448.3 1.9 collective-permute-start.11
  454.4 3.1 multiply_convert_fusion.6
  458.2 1.9 multiply_convert_fusion.7
  461.4 3.9 multiply_convert_fusion.2
  466.0 1.6 mul.751
  467.6 1.6 add_multiply_fusion
  469.2 1.8 copy.278
  471.8 3.3 collective-permute-done.10
  475.1 2.2 convert_add_fusion.5
  477.3 2.0 copy.277
  479.3 2.7 convert_add_fusion.3
  482.0 2.3 copy.273
  484.3 2.9 maximum_select_fusion
  488.3 2.3 copy.275
  490.6 5.0 reshape.285
  495.6 2.9 multiply_convert_fusion.4
  498.5 1.9 collective-permute-start.12
  500.4 3.5 convert_add_fusion
  503.9 1.7 copy.276
  505.7 3.2 multiply_convert_fusion.3
  509.0 2.6 convert_add_fusion.2
  511.6 5.9 %collective-permute-done.13 = bf16[288,576]{1,0:T(8,128)(2,1)S(1)} collective-permute-done((bf16[288,576]{1,0:T(8,128)(2,1)S(1)}, bf16[288,576]{1,0:T(8,128)(2,1)S(1)}, u32[]{:S(2)}, u32[]{:S(2)}) %collective-permute-start.13) | collective-permute-done | bytes 331808 | tf_op jit(solution)/shard_map/ppermute | solution.py:106
  (331 shorter events, 95.4 us)
Async XLA Ops:
  7.2 72.6 %all-gather.3.cloned.1.call-start = ((), (), s32[]{:S(2)}) async-start(), calls=%async_computation.8 | async-start | bytes 7206912 | tf_op jit(solution)/shard_map/all_gather | solution.py:133
  10.3 159.4 %all-gather.5.cloned.1.call-start = ((), (), s32[]{:S(2)}) async-start(), calls=%async_computation.9 | async-start | bytes 11280384 | tf_op jit(solution)/shard_map/all_gather | solution.py:142
  15.6 1.9 copy-start.56
  15.7 12.4 %copy-start.1 = (bf16[1,128,1152]{2,1,0:T(8,128)(2,1)S(1)}, bf16[1,128,1152]{2,1,0:T(8,128)(2,1)}, u32[]{:S(2)}) copy-start(bf16[1,128,1152]{2,1,0:T(8,128)(2,1)} %param.22) | copy-start | bytes 884740
  16.6 20.6 %copy-start = (f32[1152,432]{0,1:T(8,128)S(1)}, f32[1152,432]{0,1:T(8,128)}, u32[]{:S(2)}) copy-start(f32[1152,432]{0,1:T(8,128)} %param.30) | copy-start | bytes 5971972
  20.7 16.2 %all-to-all-start = ((bf16[32,2,576]{2,1,0:T(2,128)(2,1)}), bf16[32,2,576]{2,1,0:T(2,128)(2,1)S(1)}, u32[]{:S(2)}, u32[]{:S(2)}) async-start(bf16[32,2,576]{2,1,0:T(2,128)(2,1)} %reshape.313), calls=%async_computation | async-start | bytes 163840 | tf_op jit(solution)/shard_map/all_to_all | solution.py:119
  28.2 29.9 %copy-start.55 = (f32[128]{0:T(128)}, f32[128]{0:T(128)S(1)}, u32[]{:S(2)}) copy-start(f32[128]{0:T(128)S(1)} %broadcast_multiply_fusion.5) | copy-start | bytes 1540
  37.1 13.8 %copy-start.35 = (bf16[32,1,1152]{2,1,0:T(2,128)(2,1)}, bf16[32,1,1152]{2,1,0:T(2,128)(2,1)S(1)}, u32[]{:S(2)}) copy-start(bf16[32,1,1152]{2,1,0:T(2,128)(2,1)S(1)} %reshape.314) | copy-start | bytes 221188
  37.1 13.8 %copy-start.41 = (f32[16128]{0:T(1024)S(1)}, f32[16128]{0:T(1024)}, u32[]{:S(2)}) copy-start(f32[16128]{0:T(1024)} %param.31) | copy-start | bytes 193540
  46.9 11.0 %all-to-all-start.1 = ((f32[16,1,432]{2,1,0:T(1,128)}), f32[16,1,432]{2,1,0:T(1,128)S(1)}, u32[]{:S(2)}, u32[]{:S(2)}) async-start(f32[16,1,432]{2,1,0:T(1,128)} %constant_dynamic-update-slice_fusion), calls=%async_computation.1 | async-start | bytes 65536 | tf_op jit(solution)/shard_map/all_to_all | solution.py:153
  50.6 291.8 %reduce-scatter.7.cloned.1.call-start = ((), (), s32[]{:S(2)}) async-start(), calls=%async_computation.10 | async-start | bytes 5640192
  50.8 7.6 %copy-start.57 = (f32[128]{0:T(128)}, f32[128]{0:T(128)S(1)}, u32[]{:S(2)}) copy-start(f32[128]{0:T(128)S(1)} %add_rsqrt_fusion.1) | copy-start | bytes 1540
  58.4 25.3 %copy-start.19 = (bf16[128,1152]{1,0:T(8,128)(2,1)}, bf16[128,1152]{1,0:T(8,128)(2,1)S(1)}, u32[]{:S(2)}) copy-start(bf16[128,1152]{1,0:T(8,128)(2,1)S(1)} %fusion.50) | copy-start | bytes 884740
  58.4 8.4 %collective-permute-start = (bf16[128,1152]{1,0:T(8,128)(2,1)S(1)}, bf16[128,1152]{1,0:T(8,128)(2,1)S(1)}, u32[]{:S(2)}, u32[]{:S(2)}) collective-permute-start(bf16[128,1152]{1,0:T(8,128)(2,1)S(1)} %fusion.50), channel_id=1, source_target_pairs={{0,16},{16,0},{1,17},{17,1},{2,18},{18,2},{3,19},{19,3},{4,20},{20... | collective-permute-start | bytes 884744 | tf_op jit(solution)/shard_map/ppermute | solution.py:106
  66.8 12.9 %copy-start.43 = (bf16[128,1152]{1,0:T(8,128)(2,1)}, bf16[128,1152]{1,0:T(8,128)(2,1)S(1)}, u32[]{:S(2)}) copy-start(bf16[128,1152]{1,0:T(8,128)(2,1)S(1)} %collective-permute-done) | copy-start | bytes 884740
  84.3 3.1 copy-start.27
  87.4 10.0 %copy-start.23 = (bf16[2,8,72,128]{3,2,1,0:T(8,128)(2,1)}, bf16[2,8,72,128]{3,2,1,0:T(8,128)(2,1)S(1)}, u32[]{:S(2)}) copy-start(bf16[2,8,72,128]{3,2,1,0:T(8,128)(2,1)S(1)} %convolution_convert_fusion.7) | copy-start | bytes 884740
  87.4 9.2 %collective-permute-start.1 = (bf16[2,128,576]{1,2,0:T(8,128)(2,1)S(1)}, bf16[2,128,576]{1,2,0:T(8,128)(2,1)S(1)}, u32[]{:S(2)}, u32[]{:S(2)}) collective-permute-start(bf16[2,128,576]{1,2,0:T(8,128)(2,1)S(1)} %bitcast.218), channel_id=1, source_target_pairs={{0,16},{16,0},{1,17},{17,1},{2,18},{18,2},{3,19},{19,3},{4,20},{20... | collective-permute-start | bytes 884744 | tf_op jit(solution)/shard_map/ppermute | solution.py:106
  97.4 3.4 copy-start.21
  100.8 1.9 copy-start.17
  101.2 71.5 %copy-start.10 = (bf16[128,1152]{1,0:T(8,128)(2,1)}, bf16[128,1152]{1,0:T(8,128)(2,1)S(1)}, u32[]{:S(2)}) copy-start(bf16[128,1152]{1,0:T(8,128)(2,1)S(1)} %add_convert_fusion) | copy-start | bytes 884740
  101.2 9.9 %collective-permute-start.2 = (bf16[128,1152]{1,0:T(8,128)(2,1)S(1)}, bf16[128,1152]{1,0:T(8,128)(2,1)S(1)}, u32[]{:S(2)}, u32[]{:S(2)}) collective-permute-start(bf16[128,1152]{1,0:T(8,128)(2,1)S(1)} %add_convert_fusion), channel_id=1, source_target_pairs={{0,16},{16,0},{1,17},{17,1},{2,18},{18,2},{3,19},{19,3},{4,20},{20... | collective-permute-start | bytes 884744 | tf_op jit(solution)/shard_map/ppermute | solution.py:106
  103.5 73.1 %collective-permute-start.4 = (bf16[128,1152]{1,0:T(8,128)(2,1)}, bf16[128,1152]{1,0:T(8,128)(2,1)}, u32[]{:S(2)}, u32[]{:S(2)}) collective-permute-start(bf16[128,1152]{1,0:T(8,128)(2,1)} %fusion.47), channel_id=1, source_target_pairs={{0,16},{16,0},{1,17},{17,1},{2,18},{18,2},{3,19},{19,3},{4,20},{20... | collective-permute-start | bytes 884744 | tf_op jit(solution)/shard_map/ppermute | solution.py:106
  111.1 61.5 %copy-start.31 = (bf16[128,1152]{1,0:T(8,128)(2,1)}, bf16[128,1152]{1,0:T(8,128)(2,1)S(1)}, u32[]{:S(2)}) copy-start(bf16[128,1152]{1,0:T(8,128)(2,1)S(1)} %collective-permute-done.2) | copy-start | bytes 884740
  169.7 6.8 %copy-start.34 = (bf16[1152,4608]{1,0:T(8,128)(2,1)S(1)}, bf16[1152,4608]{1,0:T(8,128)(2,1)}, u32[]{:S(2)}) copy-start(bf16[1152,4608]{1,0:T(8,128)(2,1)} %all-gather.5.cloned.1.call-done) | copy-start | bytes 31850500
  172.7 13.9 %copy-start.62 = (f32[256,1152]{1,0:T(8,128)}, f32[256,1152]{1,0:T(8,128)S(1)}, u32[]{:S(2)}) copy-start(f32[256,1152]{1,0:T(8,128)S(1)} %convolution_add_fusion.3) | copy-start | bytes 3538948
  176.5 11.1 %copy-start.64 = (f32[256,1152]{1,0:T(8,128)}, f32[256,1152]{1,0:T(8,128)S(1)}, u32[]{:S(2)}) copy-start(f32[256,1152]{1,0:T(8,128)S(1)} %convolution_add_fusion.2) | copy-start | bytes 3538948
  185.0 9.9 %collective-permute-start.5 = (bf16[128,1152]{1,0:T(8,128)(2,1)S(1)}, bf16[128,1152]{1,0:T(8,128)(2,1)S(1)}, u32[]{:S(2)}, u32[]{:S(2)}) collective-permute-start(bf16[128,1152]{1,0:T(8,128)(2,1)S(1)} %slice.300), channel_id=1, source_target_pairs={{0,16},{16,0},{1,17},{17,1},{2,18},{18,2},{3,19},{19,3},{4,20},{20... | collective-permute-start | bytes 884744 | tf_op jit(solution)/shard_map/ppermute | solution.py:106
  189.1 11.4 %copy-start.12 = (f32[128,1152]{1,0:T(8,128)S(1)}, f32[128,1152]{1,0:T(8,128)}, u32[]{:S(2)}) copy-start(f32[128,1152]{1,0:T(8,128)} %get-tuple-element.250) | copy-start | bytes 1769476
  189.2 11.4 %copy-start.18 = (bf16[1,128,1152]{2,1,0:T(8,128)(2,1)S(1)}, bf16[1,128,1152]{2,1,0:T(8,128)(2,1)}, u32[]{:S(2)}) copy-start(bf16[1,128,1152]{2,1,0:T(8,128)(2,1)} %param.25) | copy-start | bytes 884740
  189.2 11.4 %collective-permute-start.3 = (bf16[128,1152]{1,0:T(8,128)(2,1)S(1)}, bf16[128,1152]{1,0:T(8,128)(2,1)S(1)}, u32[]{:S(2)}, u32[]{:S(2)}) collective-permute-start(bf16[128,1152]{1,0:T(8,128)(2,1)S(1)} %slice.301), channel_id=1, source_target_pairs={{0,16},{16,0},{1,17},{17,1},{2,18},{18,2},{3,19},{19,3},{4,20},{20... | collective-permute-start | bytes 884744 | tf_op jit(solution)/shard_map/ppermute | solution.py:106
  202.6 8.4 %copy-start.45 = (bf16[128,1152]{1,0:T(8,128)(2,1)}, bf16[128,1152]{1,0:T(8,128)(2,1)S(1)}, u32[]{:S(2)}) copy-start(bf16[128,1152]{1,0:T(8,128)(2,1)S(1)} %multiply_convert_fusion.5) | copy-start | bytes 884740
  202.6 9.1 %slice-start = ((bf16[1152,2880]{1,0:T(8,128)(2,1)}), bf16[1152,1152]{1,0:T(8,128)(2,1)S(1)}, s32[]{:S(2)}) async-start(bf16[1152,2880]{1,0:T(8,128)(2,1)} %all-gather.3.cloned.1.call-done), calls=%async_computation.12 | async-start | bytes 5308416 | tf_op jit(solution)/shard_map/slice | solution.py:134
  202.6 8.4 %collective-permute-start.6 = (bf16[128,1152]{1,0:T(8,128)(2,1)S(1)}, bf16[128,1152]{1,0:T(8,128)(2,1)S(1)}, u32[]{:S(2)}, u32[]{:S(2)}) collective-permute-start(bf16[128,1152]{1,0:T(8,128)(2,1)S(1)} %multiply_convert_fusion.5), channel_id=1, source_target_pairs={{0,16},{16,0},{1,17},{17,1},{2,18},{18,2},{3,19},{19,3},{4,20},{20... | collective-permute-start | bytes 884744 | tf_op jit(solution)/shard_map/ppermute | solution.py:106
  205.0 9.1 %copy-start.24 = (bf16[2,8,72,128]{3,2,1,0:T(8,128)(2,1)S(1)}, bf16[2,8,72,128]{3,2,1,0:T(8,128)(2,1)}, u32[]{:S(2)}) copy-start(bf16[2,8,72,128]{3,2,1,0:T(8,128)(2,1)} %copy-done.23) | copy-start | bytes 884740
  214.2 1.8 copy-start.26
  233.1 200.2 %reduce-scatter.9.cloned.1.call-start = ((), (), s32[]{:S(2)}) async-start(), calls=%async_computation.11 | async-start | bytes 11280384
  234.1 2.1 copy-start.40
  237.5 2.3 copy-start.63
  285.6 2.0 copy-start.49
  285.6 4.7 copy-start.54
  296.0 9.3 %collective-permute-start.7 = (bf16[128,1152]{1,0:T(8,128)(2,1)S(1)}, bf16[128,1152]{1,0:T(8,128)(2,1)S(1)}, u32[]{:S(2)}, u32[]{:S(2)}) collective-permute-start(bf16[128,1152]{1,0:T(8,128)(2,1)S(1)} %slice.299), channel_id=1, source_target_pairs={{0,16},{16,0},{1,17},{17,1},{2,18},{18,2},{3,19},{19,3},{4,20},{20... | collective-permute-start | bytes 884744 | tf_op jit(solution)/shard_map/ppermute | solution.py:106
  311.4 9.8 %all-to-all-start.2 = ((bf16[32,2,216]{2,1,0:T(2,128)(2,1)}), bf16[32,2,216]{2,1,0:T(2,128)(2,1)S(1)}, u32[]{:S(2)}, u32[]{:S(2)}) async-start(bf16[32,2,216]{2,1,0:T(2,128)(2,1)} %reshape.315), calls=%async_computation.2 | async-start | bytes 65536 | tf_op jit(solution)/shard_map/all_to_all | solution.py:250
  321.2 10.0 %all-to-all-start.4 = ((f32[32,1,504]{2,1,0:T(1,128)}), f32[32,1,504]{2,1,0:T(1,128)S(1)}, u32[]{:S(2)}, u32[]{:S(2)}) async-start(f32[32,1,504]{2,1,0:T(1,128)} %all_to_all.41), calls=%async_computation.4 | async-start | bytes 131072 | tf_op jit(solution)/shard_map/all_to_all | solution.py:273
  324.0 10.8 %copy-start.36 = (bf16[32,1,1152]{2,1,0:T(2,128)(2,1)S(1)}, bf16[32,1,1152]{2,1,0:T(2,128)(2,1)}, u32[]{:S(2)}) copy-start(bf16[32,1,1152]{2,1,0:T(2,128)(2,1)} %copy-done.35) | copy-start | bytes 221188
  331.2 10.5 %all-to-all-start.3 = ((f32[16,1,1152]{2,1,0:T(1,128)}), f32[16,1,1152]{2,1,0:T(1,128)S(1)}, u32[]{:S(2)}, u32[]{:S(2)}) async-start(f32[16,1,1152]{2,1,0:T(1,128)} %copy.262), calls=%async_computation.3 | async-start | bytes 147456 | tf_op jit(solution)/shard_map/all_to_all | solution.py:256
  334.8 7.0 %copy-start.51 = (f32[1,1152]{1,0:T(1,128)S(1)}, f32[1,1152]{1,0:T(1,128)}, u32[]{:S(2)}) copy-start(f32[1,1152]{1,0:T(1,128)} %get-tuple-element.210) | copy-start | bytes 13828
  334.8 7.0 %copy-start.52 = (f32[1,1152]{1,0:T(1,128)S(1)}, f32[1,1152]{1,0:T(1,128)}, u32[]{:S(2)}) copy-start(f32[1,1152]{1,0:T(1,128)} %get-tuple-element.211) | copy-start | bytes 13828
  343.7 2.0 copy-start.6
  344.1 100.0 %collective-permute-start.8 = (bf16[72,3,576]{2,1,0:T(4,128)(2,1)S(1)}, bf16[72,3,576]{2,1,0:T(4,128)(2,1)}, u32[]{:S(2)}, u32[]{:S(2)}) collective-permute-start(bf16[72,3,576]{2,1,0:T(4,128)(2,1)S(1)} %copy.264), channel_id=1, source_target_pairs={{0,16},{16,0},{1,17},{17,1},{2,18},{18,2},{3,19},{19,3},{4,20},{20... | collective-permute-start | bytes 746504 | tf_op jit(solution)/shard_map/ppermute | solution.py:106
  439.5 12.0 %all-to-all-start.5 = ((f32[32,1,505]{2,1,0:T(1,128)}), f32[32,1,505]{2,1,0:T(1,128)}, u32[]{:S(2)}, u32[]{:S(2)}) async-start(f32[32,1,505]{2,1,0:T(1,128)} %broadcast_in_dim.121), calls=%async_computation.5 | async-start | bytes 131072 | tf_op jit(solution)/shard_map/all_to_all | solution.py:119
  448.3 33.7 %collective-permute-start.11 = (bf16[72,1,4608]{2,0,1:T(8,128)(2,1)}, bf16[72,1,4608]{2,0,1:T(8,128)(2,1)}, u32[]{:S(2)}, u32[]{:S(2)}) collective-permute-start(bf16[72,1,4608]{2,0,1:T(8,128)(2,1)} %copy.272), channel_id=1, source_target_pairs={{0,16},{16,0},{1,17},{17,1},{2,18},{18,2},{3,19},{19,3},{4,20},{20... | collective-permute-start | bytes 1990664 | tf_op jit(solution)/shard_map/ppermute | solution.py:106
  453.7 4.5 copy-start.30
  454.3 3.8 copy-start.8
  454.3 3.8 copy-start.29
  454.4 7.1 %copy-start.3 = (f32[1152,432]{0,1:T(8,128)S(1)}, f32[1152,432]{0,1:T(8,128)}, u32[]{:S(2)}) copy-start(f32[1152,432]{0,1:T(8,128)} %copy-done.2) | copy-start | bytes 5971972
  457.5 3.9 copy-start.33
  457.5 21.8 %collective-permute-start.9 = (bf16[72,1728]{1,0:T(8,128)(2,1)}, bf16[72,1728]{1,0:T(8,128)(2,1)}, u32[]{:S(2)}, u32[]{:S(2)}) collective-permute-start(bf16[72,1728]{1,0:T(8,128)(2,1)} %get-tuple-element.203), channel_id=1, source_target_pairs={{0,16},{16,0},{1,17},{17,1},{2,18},{18,2},{3,19},{19,3},{4,20},{20... | collective-permute-start | bytes 746504 | tf_op jit(solution)/shard_map/ppermute | solution.py:106
  460.1 7.5 %copy-start.42 = (f32[16128]{0:T(1024)S(1)}, f32[16128]{0:T(1024)}, u32[]{:S(2)}) copy-start(f32[16128]{0:T(1024)} %param.31) | copy-start | bytes 193540
  460.1 15.0 %collective-permute-start.10 = (bf16[72,576]{0,1:T(8,128)(2,1)}, bf16[72,576]{0,1:T(8,128)(2,1)}, u32[]{:S(2)}, u32[]{:S(2)}) collective-permute-start(bf16[72,576]{0,1:T(8,128)(2,1)} %get-tuple-element.200), channel_id=1, source_target_pairs={{0,16},{16,0},{1,17},{17,1},{2,18},{18,2},{3,19},{19,3},{4,20},{20... | collective-permute-start | bytes 248840 | tf_op jit(solution)/shard_map/ppermute | solution.py:106
  465.3 35.1 %collective-permute-start.14 = (bf16[576,432]{0,1:T(8,128)(2,1)}, bf16[576,432]{0,1:T(8,128)(2,1)}, u32[]{:S(2)}, u32[]{:S(2)}) collective-permute-start(bf16[576,432]{0,1:T(8,128)(2,1)} %get-tuple-element.191), channel_id=1, source_target_pairs={{0,16},{16,0},{1,17},{17,1},{2,18},{18,2},{3,19},{19,3},{4,20},{20... | collective-permute-start | bytes 1493000 | tf_op jit(solution)/shard_map/ppermute | solution.py:106
  490.6 5.0 copy-start.5
  498.5 10.5 %collective-permute-start.12 = (bf16[72,2304]{1,0:T(8,128)(2,1)}, bf16[72,2304]{1,0:T(8,128)(2,1)}, u32[]{:S(2)}, u32[]{:S(2)}) collective-permute-start(bf16[72,2304]{1,0:T(8,128)(2,1)} %get-tuple-element.197), channel_id=1, source_target_pairs={{0,16},{16,0},{1,17},{17,1},{2,18},{18,2},{3,19},{19,3},{4,20},{20... | collective-permute-start | bytes 995336 | tf_op jit(solution)/shard_map/ppermute | solution.py:106
  508.9 8.6 %collective-permute-start.13 = (bf16[288,576]{1,0:T(8,128)(2,1)S(1)}, bf16[288,576]{1,0:T(8,128)(2,1)S(1)}, u32[]{:S(2)}, u32[]{:S(2)}) collective-permute-start(bf16[288,576]{1,0:T(8,128)(2,1)S(1)} %get-tuple-element.194), channel_id=1, source_target_pairs={{0,16},{16,0},{1,17},{17,1},{2,18},{18,2},{3,19},{19,3},{4,20},{20... | collective-permute-start | bytes 995336 | tf_op jit(solution)/shard_map/ppermute | solution.py:106
  (30 other events, 37.4 us)
Sparse Core Ops, SparseCore 0:
  10.7 69.0 all-gather.2
  82.6 87.0 all-gather.4
  233.2 76.3 reduce-scatter.6
  313.5 119.7 reduce-scatter.8
